TPU v7x, 32 devices: a whole 2x2x4 slice. The times are simulated.
32 devices in a mesh: dp: 8 (over z, y), head: 4 (over x, core).
Axes of the slice: x: 2, y: 2, z: 4, core: 2. Of those that a mesh axis runs over, the one named last changes fastest.
Arguments:
- tokens: float32 [64, 512, 768], P('dp', 'head'), may hold values from -6 to 6
- segment: int32 [64, 512], P('dp'), may hold values from 0 to 3, never falling along the last dimension, each value on 1 to 256 neighbouring positions
- modality: int32 [64, 512], P('dp', 'head'), may hold values from 0 to 1, as said below
- first_gain: float32 [2, 768], replicated, may hold values from 0.1 to 1.9
- first_shift: float32 [2, 768], replicated, may hold values from -1 to 1
- project_in: bfloat16 [768, 2304], replicated, may hold values from -0.21875 to 0.21875
- project_out: bfloat16 [768, 768], replicated, may hold values from -1.75 to 1.75
- second_gain: float32 [2, 768], replicated, may hold values from 0.1 to 1.9
- second_shift: float32 [2, 768], replicated, may hold values from -1 to 1
- up_weight: bfloat16 [2, 768, 3072], replicated, may hold values from -0.21875 to 0.21875
- down_weight: bfloat16 [2, 3072, 768], replicated, may hold values from -0.109375 to 0.109375
- cotangent: float32 [64, 512, 768], P('dp', 'head'), may hold values from -6 to 6
Outputs:
- output: float32 [64, 512, 768], P('dp', 'head')
- input_grad: float32 [64, 512, 768], P('dp', 'head')
- first_gain_grad: float32 [2, 768], P(None, 'dp')
- first_shift_grad: float32 [2, 768], P(None, 'dp')
- project_in_grad: float32 [768, 2304], P('dp')
- project_out_grad: float32 [768, 768], P('dp')
- second_gain_grad: float32 [2, 768], P(None, 'dp')
- second_shift_grad: float32 [2, 768], P(None, 'dp')
- up_weight_grad: float32 [2, 768, 3072], P(None, 'dp')
- down_weight_grad: float32 [2, 3072, 768], P(None, 'dp')
Inputs may be any that keep to these rules, and one draw needn't show every extreme that they name: Along each row segment numbers never fall; each segment is a run of 1 to 256 positions, and some run has exactly that many. On every device exactly 640 of its 1024 tokens have one modality and the others have the other one; which one is the larger varies by device.
All inputs are finite; a program needn't handle non-finite values.
Results may differ from a plain program's by a relative error of at most 0.015.
Values may be sent and summed in bfloat16 or wider, within the bound.
A program may use at most 320 MiB of HBM per device.

v0:
```python
import jax
import jax.numpy as jnp
from jax import lax
from jax.sharding import PartitionSpec as P

HEAD_DIM = 64
EXPERTS = 2
epsilon = 1e-05


def layer_norm(inputs, gains, shifts):
    centered = inputs - jnp.mean(inputs, axis=-1, keepdims=True)
    variance = jnp.mean(centered * centered, axis=-1, keepdims=True)
    return centered * lax.rsqrt(variance + epsilon) * gains + shifts


def pick(expert_table, token_kind):
    return jnp.where(token_kind[:, None] == 0, expert_table[0], expert_table[1])


def by_expert(per_token, token_kind):
    return jnp.stack(
        [
            jnp.sum(jnp.where(token_kind[:, None] == expert, per_token, 0.0), axis=0)
            for expert in range(EXPERTS)
        ]
    )


def gelu_exact(inputs):
    return jax.nn.gelu(inputs, approximate=False)


def body(
    tokens,
    segment,
    modality,
    first_gain,
    first_shift,
    project_in,
    project_out,
    second_gain,
    second_shift,
    up_weight,
    down_weight,
    cotangent,
):
    row_count, local_len, model_width = tokens.shape
    seq_len = segment.shape[1]
    token_count = row_count * local_len
    query_scale = HEAD_DIM ** (-0.5)
    flat_tokens = tokens.reshape(token_count, model_width)
    token_kind = modality.reshape(token_count)
    first_normed, first_back = jax.vjp(
        layer_norm, flat_tokens, pick(first_gain, token_kind), pick(first_shift, token_kind)
    )
    first_low = first_normed.astype(jnp.bfloat16)
    projected = jnp.dot(first_low, project_in, preferred_element_type=jnp.float32).astype(
        jnp.bfloat16
    )
    head_side = lax.all_to_all(
        projected.reshape(row_count, local_len, 3, model_width),
        "head",
        split_axis=3,
        concat_axis=1,
        tiled=True,
    )
    attend_rows = head_side.shape[0]
    heads_here = head_side.shape[3] // HEAD_DIM
    query = head_side[:, :, 0].reshape(attend_rows, seq_len, heads_here, HEAD_DIM) * query_scale
    keys = head_side[:, :, 1].reshape(attend_rows, seq_len, heads_here, HEAD_DIM)
    values = head_side[:, :, 2].reshape(attend_rows, seq_len, heads_here, HEAD_DIM)
    same_segment = (segment[:, :, None] == segment[:, None, :])[:, None]

    def masked_scores(query, keys):
        scores = jnp.einsum("rqhc,rkhc->rhqk", query, keys, preferred_element_type=jnp.float32)
        return jnp.where(same_segment, scores, -1000000000.0)

    masked = masked_scores(query, keys)
    peak = jnp.max(masked, axis=-1, keepdims=True)
    expanded = jnp.exp(masked - peak)
    totals = jnp.sum(expanded, axis=-1, keepdims=True)
    probs = expanded / totals
    log_total = peak + jnp.log(totals)
    context = jnp.einsum(
        "rhqk,rkhc->rqhc", probs.astype(jnp.bfloat16), values, preferred_element_type=jnp.float32
    )
    context = context.astype(jnp.bfloat16).reshape(attend_rows, seq_len, heads_here * HEAD_DIM)
    context_tok = lax.all_to_all(context, "head", split_axis=1, concat_axis=2, tiled=True)
    context_flat = context_tok.reshape(token_count, model_width)
    attention = jnp.dot(context_flat, project_out, preferred_element_type=jnp.float32)
    residual = flat_tokens + attention
    second_normed, second_back = jax.vjp(
        layer_norm, residual, pick(second_gain, token_kind), pick(second_shift, token_kind)
    )
    second_low = second_normed.astype(jnp.bfloat16)
    order = jnp.argsort(token_kind, stable=True)
    capacity = 5 * token_count // 8
    slot_sets = (order[:capacity], order[token_count - capacity :])
    branch_sum = jnp.zeros((token_count, model_width), jnp.float32)
    kept_items = []
    for expert in range(EXPERTS):
        slots = slot_sets[expert]
        live_rows = (token_kind[slots] == expert)[:, None]
        hidden = jnp.dot(second_low[slots], up_weight[expert], preferred_element_type=jnp.float32)
        activated, gelu_back = jax.vjp(gelu_exact, hidden)
        active_low = activated.astype(jnp.bfloat16)
        branch = jnp.dot(active_low, down_weight[expert], preferred_element_type=jnp.float32)
        branch_sum = branch_sum.at[slots].add(jnp.where(live_rows, branch, 0.0))
        kept_items.append((slots, live_rows, active_low, gelu_back))
    output = residual + branch_sum
    out_grad_flat = cotangent.reshape(token_count, model_width)
    grad_low = out_grad_flat.astype(jnp.bfloat16)
    second_grad = jnp.zeros((token_count, model_width), jnp.float32)
    up_terms = []
    down_terms = []
    for expert in range(EXPERTS):
        slots, live_rows, active_low, gelu_back = kept_items[expert]
        branch_grad = jnp.where(live_rows, grad_low[slots], jnp.zeros((), jnp.bfloat16))
        down_terms.append(
            jnp.einsum("tf,td->fd", active_low, branch_grad, preferred_element_type=jnp.float32)
        )
        active_grad = jnp.einsum(
            "td,fd->tf", branch_grad, down_weight[expert], preferred_element_type=jnp.float32
        )
        hidden_grad = gelu_back(active_grad)[0].astype(jnp.bfloat16)
        up_terms.append(
            jnp.einsum(
                "td,tf->df", second_low[slots], hidden_grad, preferred_element_type=jnp.float32
            )
        )
        second_grad = second_grad.at[slots].add(
            jnp.einsum(
                "tf,df->td", hidden_grad, up_weight[expert], preferred_element_type=jnp.float32
            )
        )
    residual_norm_grad, second_gain_tok, second_shift_tok = second_back(second_grad)
    second_gain_term = by_expert(second_gain_tok, token_kind)
    second_shift_term = by_expert(second_shift_tok, token_kind)
    up_term = jnp.stack(up_terms)
    down_term = jnp.stack(down_terms)
    residual_grad = out_grad_flat + residual_norm_grad
    attention_low = residual_grad.astype(jnp.bfloat16)
    out_term = jnp.einsum(
        "td,te->de", context_flat, attention_low, preferred_element_type=jnp.float32
    )
    context_grad = jnp.einsum(
        "te,de->td", attention_low, project_out, preferred_element_type=jnp.float32
    ).astype(jnp.bfloat16)
    context_grad = context_grad.reshape(row_count, local_len, model_width)
    context_heads = lax.all_to_all(context_grad, "head", split_axis=2, concat_axis=1, tiled=True)
    grad_heads = context_heads.reshape(attend_rows, seq_len, heads_here, HEAD_DIM)
    again = jnp.exp(masked_scores(query, keys) - log_total)
    prob_grad = jnp.einsum(
        "rqhc,rkhc->rhqk", grad_heads, values, preferred_element_type=jnp.float32
    )
    score_grad = (again * (prob_grad - jnp.sum(again * prob_grad, axis=-1, keepdims=True))).astype(
        jnp.bfloat16
    )
    query_grad = (
        jnp.einsum("rhqk,rkhc->rqhc", score_grad, keys, preferred_element_type=jnp.float32)
        * query_scale
    )
    keys_grad = jnp.einsum("rhqk,rqhc->rkhc", score_grad, query, preferred_element_type=jnp.float32)
    values_grad = jnp.einsum(
        "rhqk,rqhc->rkhc",
        again.astype(jnp.bfloat16),
        grad_heads,
        preferred_element_type=jnp.float32,
    )
    projected_grad = jnp.stack([query_grad, keys_grad, values_grad], axis=2).astype(jnp.bfloat16)
    projected_grad = projected_grad.reshape(attend_rows, seq_len, 3, heads_here * HEAD_DIM)
    grads_tok = lax.all_to_all(
        projected_grad, "head", split_axis=1, concat_axis=3, tiled=True
    ).reshape(token_count, 3 * model_width)
    first_grad = jnp.einsum("tf,df->td", grads_tok, project_in, preferred_element_type=jnp.float32)
    in_term = jnp.einsum("td,tf->df", first_low, grads_tok, preferred_element_type=jnp.float32)
    input_norm_grad, first_gain_tok, first_shift_tok = first_back(first_grad)
    input_grad = residual_grad + input_norm_grad
    first_gain_term = by_expert(first_gain_tok, token_kind)
    first_shift_term = by_expert(first_shift_tok, token_kind)
    weight_part = (
        lax.psum_scatter(first_gain_term, "dp", scatter_dimension=1, tiled=True),
        lax.psum_scatter(first_shift_term, "dp", scatter_dimension=1, tiled=True),
        lax.psum_scatter(in_term, "dp", scatter_dimension=0, tiled=True),
        lax.psum_scatter(out_term, "dp", scatter_dimension=0, tiled=True),
        lax.psum_scatter(second_gain_term, "dp", scatter_dimension=1, tiled=True),
        lax.psum_scatter(second_shift_term, "dp", scatter_dimension=1, tiled=True),
        lax.psum_scatter(up_term, "dp", scatter_dimension=1, tiled=True),
        lax.psum_scatter(down_term, "dp", scatter_dimension=1, tiled=True),
    )
    weight_sums = (
        lax.psum(weight_part[0].astype(jnp.bfloat16), "head").astype(jnp.float32),
        lax.psum(weight_part[1].astype(jnp.bfloat16), "head").astype(jnp.float32),
        lax.psum(weight_part[2].astype(jnp.bfloat16), "head").astype(jnp.float32),
        lax.psum(weight_part[3].astype(jnp.bfloat16), "head").astype(jnp.float32),
        lax.psum(weight_part[4].astype(jnp.bfloat16), "head").astype(jnp.float32),
        lax.psum(weight_part[5].astype(jnp.bfloat16), "head").astype(jnp.float32),
        lax.psum(weight_part[6].astype(jnp.bfloat16), "head").astype(jnp.float32),
        lax.psum(weight_part[7].astype(jnp.bfloat16), "head").astype(jnp.float32),
    )
    attention_sums = weight_sums[:4]
    expert_sums = weight_sums[4:]
    return (
        output.reshape(row_count, local_len, model_width),
        input_grad.reshape(row_count, local_len, model_width),
        attention_sums[0],
        attention_sums[1],
        attention_sums[2],
        attention_sums[3],
        expert_sums[0],
        expert_sums[1],
        expert_sums[2],
        expert_sums[3],
    )


def solution(mesh):
    return jax.shard_map(
        body,
        mesh=mesh,
        in_specs=(
            P("dp", "head", None),
            P("dp", None),
            P("dp", "head"),
            P(),
            P(),
            P(),
            P(),
            P(),
            P(),
            P(),
            P(),
            P("dp", "head", None),
        ),
        out_specs=(
            P("dp", "head", None),
            P("dp", "head", None),
            P(None, "dp"),
            P(None, "dp"),
            P("dp", None),
            P("dp", None),
            P(None, "dp"),
            P(None, "dp"),
            P(None, "dp", None),
            P(None, "dp", None),
        ),
        check_vma=False,
    )
```

profile of v0, /device:TPU:0, one launch (start us, length us, event | category | flops | bytes accessed | tf_op | source)
XLA Modules:
  0.0 1643.8 jit_solution(14196574063786381380)
XLA Ops:
  15.7 5.5 convolution_convert_fusion
  21.2 11.3 reshape.308
  32.5 7.6 copy.70
  52.7 47.0 %all-to-all-done = bf16[8,128,3,768]{1,0,2,3:T(8,128)(2,1)} async-done(((bf16[8,128,3,768]{1,0,2,3:T(8,128)(2,1)}), bf16[8,128,3,768]{1,0,2,3:T(8,128)(2,1)}, u32[]{:S(2)}, u32[]{:S(2)}) %all-to-all-start) | async-done | bytes 4718624 | tf_op jit(solution)/shard_map/all_to_all | solution.py:61
  99.7 8.1 copy.72
  107.9 8.0 all_to_all.49
  118.9 10.5 select_reduce_fusion
  129.5 11.4 fusion
  140.9 12.4 fusion.62
  170.6 5.5 gather_fusion.5
  180.6 5.5 gather_fusion.4
  205.1 5.5 gather_fusion.3
  210.7 5.5 gather_fusion.1
  216.2 23.3 %multiply_convert_fusion.1 = (bf16[640,3072]{1,0:T(8,128)(2,1)}, f32[640,3072]{1,0:T(8,128)}, f32[640,3072]{1,0:T(8,128)}) fusion(bf16[640,768]{1,0:T(8,128)(2,1)} %gather_fusion.3, bf16[2,768,3072]{2,1,0:T(8,128)(2,1)} %param.21), kind=kOutput, calls=%fused_computation.31 | convolution fusion | flops 3147694080 | bytes 25362432 | tf_op jit(solution)/shard_map/dot_general | solution.py:105
  239.6 22.6 %multiply_convert_fusion.2 = (bf16[640,3072]{1,0:T(8,128)(2,1)}, f32[640,3072]{1,0:T(8,128)}, f32[640,3072]{1,0:T(8,128)}) fusion(bf16[640,768]{1,0:T(8,128)(2,1)S(1)} %copy-done.23, bf16[2,768,3072]{2,1,0:T(8,128)(2,1)} %param.21), kind=kOutput, calls=%fused_computation.44 | convolution fusion | flops 3147694080 | bytes 25362432 | tf_op jit(solution)/shard_map/dot_general | solution.py:105
  262.2 10.0 add_convert_fusion
  276.8 9.9 add_convert_fusion.1
  293.2 9.8 scatter_custom_fusion.2
  303.0 11.7 scatter_fusion
  340.5 13.4 all-to-all-done.2
  361.8 19.9 %multiply_reduce_fusion = (f32[8,3,512]{2,1,0:T(4,128)S(1)}, f32[8,3,512,512]{2,3,1,0:T(8,128)}) fusion(f32[8,3,512,512]{2,3,1,0:T(8,128)} %get-tuple-element.56, f32[8,3,512]{2,1,0:T(4,128)} %log_add_fusion, pred[8,512,512]{1,2,0:T(8,128)(4,1)} %broadcast_compare_fusion, bf16[8,512,3,64]{1,3,2,0:T(8,128)(2,1)} %reshape.215, ...), kind=kOutput, calls=%fused_computation.11 | convolution fusion | flops 830459904 | bytes 55672832 | tf_op jit(solution)/shard_map/rqhc,rkhc->rhqk/dot_general | solution.py:154
  381.7 17.6 %multiply_convert_fusion = bf16[8,3,512,512]{2,3,1,0:T(8,128)(2,1)S(1)} fusion(f32[8,3,512,512]{2,3,1,0:T(8,128)} %get-tuple-element.62, f32[8,3,512,512]{2,3,1,0:T(8,128)} %get-tuple-element.56, f32[8,3,512]{2,1,0:T(4,128)S(1)} %get-tuple-element.61, f32[8,3,512]{2,1,0:T(4,128)S(1)} %copy-done.31, pred[8,512,512]{1,2,0:T(8,128)(4,1)S(1)} %copy-done.7), kind=kLoop, calls=%fused_computation.10 | loop fusion | flops 31457280 | bytes 65110016 | tf_op jit(solution)/shard_map/convert_element_type | solution.py:157
  407.2 9.8 convolution_convert_fusion.1
  417.1 13.1 fusion.63
  443.5 6.7 pad_maximum_fusion.2
  450.2 5.2 all-to-all-start.3
  459.1 67.0 %all-to-all-done.3 = bf16[8,512,3,192]{3,0,2,1:T(8,128)(2,1)} async-done(((bf16[8,512,3,192]{3,0,2,1:T(8,128)(2,1)}), bf16[8,512,3,192]{3,0,2,1:T(8,128)(2,1)}, u32[]{:S(2)}, u32[]{:S(2)}) %all-to-all-start.3) | async-done | bytes 4718624 | tf_op jit(solution)/shard_map/all_to_all | solution.py:173
  526.1 8.6 copy.97
  534.7 5.5 copy.87
  542.4 5.9 fusion.20
  548.6 6.4 convolution_bitcast_fusion.2
  559.0 7.0 pad_maximum_fusion
  566.6 6.5 convolution_bitcast_fusion
  577.2 6.9 pad_maximum_fusion.1
  593.9 11.0 select_reduce_fusion.8
  612.9 8.2 fusion.34
  622.7 56.0 %reduce-scatter.17.cloned.1.call-done = f32[96,2304]{1,0:T(8,128)} async-done(((f32[768,2304]{1,0:T(8,128)}), f32[96,2304]{1,0:T(8,128)}) %reduce-scatter.17.cloned.1.call-update) | async-done | bytes 884752 | tf_op jit(solution)/shard_map/reduce_scatter | solution.py:185
  680.6 310.8 %reduce-scatter.21.cloned.1.call-done = f32[2,96,3072]{2,1,0:T(8,128)} async-done(((f32[2,768,3072]{2,1,0:T(8,128)}), f32[2,96,3072]{2,1,0:T(8,128)}) %reduce-scatter.21.cloned.1.call-update) | async-done | bytes 2359312 | tf_op jit(solution)/shard_map/reduce_scatter | solution.py:189
  994.2 309.7 %reduce-scatter.23.cloned.1.call-done = f32[2,384,768]{2,1,0:T(8,128)} async-done(((f32[2,3072,768]{2,1,0:T(8,128)}), f32[2,384,768]{2,1,0:T(8,128)}) %reduce-scatter.23.cloned.1.call-update) | async-done | bytes 2359312 | tf_op jit(solution)/shard_map/reduce_scatter | solution.py:190
  1306.8 8.0 fusion.26
  1314.8 12.2 scatter_custom_fusion
  1327.0 12.1 scatter_custom_fusion.1
  1339.1 29.3 %reduce-scatter.31.cloned.1.call-done = f32[96,2]{1,0:T(8,128)} async-done(((f32[768,2]{1,0:T(8,128)}), f32[96,2]{1,0:T(8,128)}) %reduce-scatter.31.cloned.1.call-update) | async-done | bytes 784
  1369.8 63.0 %reduce-scatter.29.cloned.1.call-done = f32[96,2]{1,0:T(8,128)} async-done(((f32[768,2]{1,0:T(8,128)}), f32[96,2]{1,0:T(8,128)}) %reduce-scatter.29.cloned.1.call-update) | async-done | bytes 784
  1440.9 56.5 %reduce-scatter.27.cloned.1.call-done = f32[96,2]{1,0:T(8,128)} async-done(((f32[768,2]{1,0:T(8,128)}), f32[96,2]{1,0:T(8,128)}) %reduce-scatter.27.cloned.1.call-update) | async-done | bytes 784
  1498.3 63.7 %reduce-scatter.25.cloned.1.call-done = f32[96,2]{1,0:T(8,128)} async-done(((f32[768,2]{1,0:T(8,128)}), f32[96,2]{1,0:T(8,128)}) %reduce-scatter.25.cloned.1.call-update) | async-done | bytes 784
  1562.9 6.2 all-reduce
  1574.0 55.6 %all-reduce.4.cloned.1.call-done = (bf16[96,2304]{1,0:T(8,128)(2,1)}, bf16[96,768]{1,0:T(8,128)(2,1)}, bf16[2,96,3072]{2,1,0:T(8,128)(2,1)}, bf16[2,384,768]{2,1,0:T(8,128)(2,1)}) async-done(((bf16[96,2304]{1,0:T(8,128)(2,1)}, bf16[96,768]{1,0:T(8,128)(2,1)}, bf16[2,96,3072]{2,1,0:T(8,128)(2,1)}, bf16[2,384,768]{2,1,0:T(8,128)(2,1)}), (bf16[96,2304]{1,0:T(8,128)(2,1)}, bf16[96,768]{1,0:T(8,128)(2,1)}, ...) | async-done | bytes 2949136 | tf_op jit(solution)/shard_map/psum | solution.py:195
  (261 shorter events, 195.6 us)
Async XLA Ops:
  7.2 8.5 copy-start
  40.1 59.6 %all-to-all-start = ((bf16[8,128,3,768]{1,0,2,3:T(8,128)(2,1)}), bf16[8,128,3,768]{1,0,2,3:T(8,128)(2,1)}, u32[]{:S(2)}, u32[]{:S(2)}) async-start(bf16[8,128,3,768]{1,0,2,3:T(8,128)(2,1)} %copy.70), calls=%async_computation | async-start | bytes 9437184 | tf_op jit(solution)/shard_map/all_to_all | solution.py:61
  118.7 10.7 copy-start.10
  118.7 10.7 copy-start.12
  118.7 22.1 %copy-start.17 = (bf16[8,512,1,192]{1,3,2,0:T(8,128)(2,1)}, bf16[8,512,1,192]{1,3,2,0:T(8,128)(2,1)S(1)}, u32[]{:S(2)}) copy-start(bf16[8,512,1,192]{1,3,2,0:T(8,128)(2,1)S(1)} %get-tuple-element.48) | copy-start | bytes 4718596
  129.5 11.4 copy-start.30
  140.9 12.4 copy-start.33
  157.9 32.2 %all-to-all-start.1 = ((bf16[8,512,192]{2,0,1:T(8,128)(2,1)}), bf16[8,512,192]{2,0,1:T(8,128)(2,1)}, u32[]{:S(2)}, u32[]{:S(2)}) async-start(bf16[8,512,192]{2,0,1:T(8,128)(2,1)} %copy.74), calls=%async_computation.1 | async-start | bytes 4194304 | tf_op jit(solution)/shard_map/all_to_all | solution.py:89
  162.4 13.8 copy-start.51
  187.6 14.7 copy-start.39
  187.6 14.7 copy-start.41
  196.2 6.6 copy-start.59
  196.2 6.6 copy-start.62
  196.2 6.6 copy-start.63
  216.2 23.4 %copy-start.23 = (bf16[640,768]{1,0:T(8,128)(2,1)S(1)}, bf16[640,768]{1,0:T(8,128)(2,1)}, u32[]{:S(2)}) copy-start(bf16[640,768]{1,0:T(8,128)(2,1)} %gather_fusion.1) | copy-start | bytes 2949124
  216.2 56.0 %slice-start = ((s8[9437184]{0:T(1024)(128)(4,1)}), s8[4194304]{0:T(1024)(128)(4,1)S(1)}, s32[]{:S(2)}) async-start(s8[9437184]{0:T(1024)(128)(4,1)} %bitcast.193), calls=%async_computation.21 | async-start | bytes 8388608
  216.2 56.0 %slice-start.1 = ((s8[9437184]{0:T(1024)(128)(4,1)}), s8[4194304]{0:T(1024)(128)(4,1)S(1)}, s32[]{:S(2)}) async-start(s8[9437184]{0:T(1024)(128)(4,1)} %bitcast.193), calls=%async_computation.22 | async-start | bytes 8388608
  239.6 22.6 %copy-start.27 = (bf16[640,768]{1,0:T(8,128)(2,1)S(1)}, bf16[640,768]{1,0:T(8,128)(2,1)}, u32[]{:S(2)}) copy-start(bf16[640,768]{1,0:T(8,128)(2,1)} %gather_fusion.5) | copy-start | bytes 2949124
  239.6 22.6 %copy-start.65 = (pred[640]{0:T(1024)(128)(4,1)S(1)}, pred[640]{0:T(1024)(128)(4,1)}, u32[]{:S(2)}) copy-start(pred[640]{0:T(1024)(128)(4,1)} %broadcast_compare_fusion.3) | copy-start | bytes 1924
  239.6 32.7 %slice-start.2 = ((s8[9437184]{0:T(1024)(128)(4,1)}), s8[1048576]{0:T(1024)(128)(4,1)S(1)}, s32[]{:S(2)}) async-start(s8[9437184]{0:T(1024)(128)(4,1)} %bitcast.193), calls=%async_computation.23 | async-start | bytes 2097152
  303.0 11.7 copy-start.36
  303.0 11.7 copy-start.40
  303.0 11.7 copy-start.42
  303.0 11.7 copy-start.44
  329.4 24.5 %all-to-all-start.2 = ((bf16[8,128,768]{1,0,2:T(8,128)(2,1)}), bf16[8,128,768]{1,0,2:T(8,128)(2,1)}, u32[]{:S(2)}, u32[]{:S(2)}) async-start(bf16[8,128,768]{1,0,2:T(8,128)(2,1)} %copy.77), calls=%async_computation.2 | async-start | bytes 3145728 | tf_op jit(solution)/shard_map/all_to_all | solution.py:151
  333.7 287.3 %reduce-scatter.19.cloned.1.call-start = ((), (), s32[]{:S(2)}) async-start(), calls=%async_computation.13 | async-start | bytes 2654208 | tf_op jit(solution)/shard_map/reduce_scatter | solution.py:186
  361.8 19.9 %copy-start.7 = (pred[8,512,512]{1,2,0:T(8,128)(4,1)S(1)}, pred[8,512,512]{1,2,0:T(8,128)(4,1)}, u32[]{:S(2)}) copy-start(pred[8,512,512]{1,2,0:T(8,128)(4,1)} %broadcast_compare_fusion) | copy-start | bytes 6291460
  361.8 19.9 %copy-start.31 = (f32[8,3,512]{2,1,0:T(4,128)S(1)}, f32[8,3,512]{2,1,0:T(4,128)}, u32[]{:S(2)}) copy-start(f32[8,3,512]{2,1,0:T(4,128)} %log_add_fusion) | copy-start | bytes 147460
  381.7 22.2 %copy-start.13 = (bf16[8,512,1,192]{1,3,2,0:T(8,128)(2,1)S(1)}, bf16[8,512,1,192]{1,3,2,0:T(8,128)(2,1)}, u32[]{:S(2)}) copy-start(bf16[8,512,1,192]{1,3,2,0:T(8,128)(2,1)} %copy-done.12) | copy-start | bytes 4718596
  407.2 9.9 copy-start.18
  450.2 75.9 %all-to-all-start.3 = ((bf16[8,512,3,192]{3,0,2,1:T(8,128)(2,1)}), bf16[8,512,3,192]{3,0,2,1:T(8,128)(2,1)}, u32[]{:S(2)}, u32[]{:S(2)}) async-start(bf16[8,512,3,192]{3,0,2,1:T(8,128)(2,1)} %pad_maximum_fusion.2), calls=%async_computation.3 | async-start | bytes 12582912 | tf_op jit(solution)/shard_map/all_to_all | solution.py:173
  455.5 223.2 %reduce-scatter.17.cloned.1.call-start = ((), (), s32[]{:S(2)}) async-start(), calls=%async_computation.12 | async-start | bytes 7962624 | tf_op jit(solution)/shard_map/reduce_scatter | solution.py:185
  534.7 7.7 copy-start.26
  548.3 443.1 %reduce-scatter.21.cloned.1.call-start = ((), (), s32[]{:S(2)}) async-start(), calls=%async_computation.14 | async-start | bytes 21233664 | tf_op jit(solution)/shard_map/reduce_scatter | solution.py:189
  548.6 6.5 copy-start.22
  566.0 738.0 %reduce-scatter.23.cloned.1.call-start = ((), (), s32[]{:S(2)}) async-start(), calls=%async_computation.15 | async-start | bytes 21233664 | tf_op jit(solution)/shard_map/reduce_scatter | solution.py:190
  566.6 6.5 copy-start.29
  566.6 6.5 copy-start.68
  566.6 6.5 copy-start.72
  584.1 9.8 copy-start.53
  584.1 784.3 %reduce-scatter.31.cloned.1.call-start = ((), (), s32[]{:S(2)}) async-start(), calls=%async_computation.19 | async-start | bytes 442368
  590.3 842.5 %reduce-scatter.29.cloned.1.call-start = ((), (), s32[]{:S(2)}) async-start(), calls=%async_computation.18 | async-start | bytes 442368
  593.4 904.1 %reduce-scatter.27.cloned.1.call-start = ((), (), s32[]{:S(2)}) async-start(), calls=%async_computation.17 | async-start | bytes 442368
  609.7 952.3 %reduce-scatter.25.cloned.1.call-start = ((), (), s32[]{:S(2)}) async-start(), calls=%async_computation.16 | async-start | bytes 442368
  612.7 1016.9 %all-reduce.4.cloned.1.call-start = ((), (), s32[]{:S(2)}) async-start(), calls=%async_computation.20 | async-start | bytes 5898240 | tf_op jit(solution)/shard_map/psum | solution.py:195
  1438.9 124.0 %copy-start.69 = (bf16[2,96]{1,0:T(2,128)(2,1)S(1)}, bf16[2,96]{1,0:T(2,128)(2,1)}, u32[]{:S(2)}) copy-start(bf16[2,96]{1,0:T(2,128)(2,1)} %copy.105) | copy-start | bytes 1156
  1438.9 124.0 %copy-start.70 = (bf16[2,96]{1,0:T(2,128)(2,1)S(1)}, bf16[2,96]{1,0:T(2,128)(2,1)}, u32[]{:S(2)}) copy-start(bf16[2,96]{1,0:T(2,128)(2,1)} %copy.103) | copy-start | bytes 1156
  1629.5 6.8 copy-start.34
  (41 other events, 132.6 us)
Sparse Core Ops, SparseCore 0:
  340.6 72.0 reduce-scatter.18
  548.4 130.1 reduce-scatter.16
  682.5 308.8 reduce-scatter.20
  995.1 308.8 reduce-scatter.22
  1307.1 61.3 reduce-scatter.30
  1371.6 61.2 reduce-scatter.28
  1436.1 61.2 reduce-scatter.26
  1500.7 61.2 reduce-scatter.24
  1565.2 64.3 all-reduce.3
where the time goes:
time: 1650 us; the launch traced here: 1640 us
  waiting for transfers between devices  1070 us (65%)
  matrix products  216 us (13%)
  other arithmetic  166 us (10%)
  local copies, waits for them, and re-layouts  149 us (9%)
  starting transfers between devices  20.7 us (1%)
    reduce_scatter x1, waiting for transfers between devices, body(): lax.psum_scatter(up_term, 'dp', scatter_dimension=1, tiled=True)  311 us
    reduce_scatter x1, waiting for transfers between devices, body(): lax.psum_scatter(down_term, 'dp', scatter_dimension=1, tiled=True)  310 us
    unnamed x13, waiting for transfers between devices  213 us
    all_to_all x1, waiting for transfers between devices, body(): lax.all_to_all(projected_grad, 'head', split_axis=1, concat_axis=3, tiled...  67 us
    reduce_scatter x1, waiting for transfers between devices, body(): lax.psum_scatter(in_term, 'dp', scatter_dimension=0, tiled=True)  56 us
    psum x1, waiting for transfers between devices, body(): lax.psum(weight_part[2].astype(jnp.bfloat16), 'head').astype(jnp.float32)  55.6 us
    all_to_all x1, waiting for transfers between devices, body(): lax.all_to_all(projected.reshape(row_count, local_len, 3, model_width), '...  47 us
    dot_general x2, matrix products, body(): jnp.dot(second_low[slots], up_weight[expert], preferred_element_type=jnp....  45.9 us
  transfers between devices with their start and end apart: 13, of which 11 were waited for; matrix products, arithmetic and copies ran while one was open for 17% of the time, Pallas kernels for 0%

commit v1 on v0

--- a/solution.py
+++ b/solution.py
@@ -6,6 +6,28 @@
 HEAD_DIM = 64
 EXPERTS = 2
 epsilon = 1e-05
+
+
+def split_up(shard, dim, count):
+    before, after = (shard.shape[:dim], shard.shape[dim + 1 :])
+    return jnp.moveaxis(shard.reshape(*before, count, -1, *after), dim, 0)
+
+
+def joined_along(tiles, dim):
+    shape = list(tiles.shape[1:])
+    shape[dim] *= tiles.shape[0]
+    return jnp.moveaxis(tiles, 0, dim).reshape(shape)
+
+
+def exchange_in_pairs(shard, axis, split_dim, concat_dim):
+    size, here = (lax.axis_size(axis), lax.axis_index(axis))
+    blocks = split_up(shard, split_dim, size)
+    done = [blocks[here]]
+    for turn in range(1, size):
+        sent = blocks[here ^ turn]
+        done.append(lax.ppermute(sent, axis, [(i, i ^ turn) for i in range(size)]))
+    blocks = jnp.stack(done)[here ^ jnp.arange(size)]
+    return joined_along(blocks, concat_dim)
 
 
 def layer_norm(inputs, gains, shifts):
@@ -58,12 +80,8 @@
     projected = jnp.dot(first_low, project_in, preferred_element_type=jnp.float32).astype(
         jnp.bfloat16
     )
-    head_side = lax.all_to_all(
-        projected.reshape(row_count, local_len, 3, model_width),
-        "head",
-        split_axis=3,
-        concat_axis=1,
-        tiled=True,
+    head_side = exchange_in_pairs(
+        projected.reshape(row_count, local_len, 3, model_width), "head", 3, 1
     )
     attend_rows = head_side.shape[0]
     heads_here = head_side.shape[3] // HEAD_DIM

time: 1650 us -> 1640 us (level)
    all_to_all x1 -> x0, waiting for transfers between devices: 47 us -> none  [body(): lax.all_to_all(projected.reshape(row_count, local_len, 3, model_width), '...]
    ppermute x0 -> x3, waiting for transfers between devices: none -> 40 us  [exchange_in_pairs(): done.append(lax.ppermute(sent, axis, [(i, i ^ turn) for i in range(size)]))]
  transfers between devices with their start and end apart: 13 -> 15, of which waited for: 11 -> 12; matrix products, arithmetic and copies ran while one was open for 17% -> 18% of each run, Pallas kernels for 0% -> 0%
where the time goes in v1:
time: 1640 us; the launch traced here: 1630 us
  waiting for transfers between devices  1060 us (65%)
  matrix products  216 us (13%)
  other arithmetic  167 us (10%)
  local copies, waits for them, and re-layouts  144 us (9%)
  starting transfers between devices  18.7 us (1%)
    reduce_scatter x1, waiting for transfers between devices, body(): lax.psum_scatter(up_term, 'dp', scatter_dimension=1, tiled=True)  311 us
    reduce_scatter x1, waiting for transfers between devices, body(): lax.psum_scatter(down_term, 'dp', scatter_dimension=1, tiled=True)  310 us
    unnamed x13, waiting for transfers between devices  213 us
    all_to_all x1, waiting for transfers between devices, body(): lax.all_to_all(projected_grad, 'head', split_axis=1, concat_axis=3, tiled...  67 us
    reduce_scatter x1, waiting for transfers between devices, body(): lax.psum_scatter(in_term, 'dp', scatter_dimension=0, tiled=True)  55.8 us
    psum x1, waiting for transfers between devices, body(): lax.psum(weight_part[2].astype(jnp.bfloat16), 'head').astype(jnp.float32)  55.6 us
    dot_general x2, matrix products, body(): jnp.dot(second_low[slots], up_weight[expert], preferred_element_type=jnp....  46.1 us
    ppermute x3, waiting for transfers between devices, exchange_in_pairs(): done.append(lax.ppermute(sent, axis, [(i, i ^ turn) for i in range(size)]))  40 us
  transfers between devices with their start and end apart: 15, of which 12 were waited for; matrix products, arithmetic and copies ran while one was open for 18% of the time, Pallas kernels for 0%

profile of v1, /device:TPU:0, one launch (start us, length us, event | category | flops | bytes accessed | tf_op | source)
XLA Modules:
  0.0 1631.8 jit_solution(4828476635316545702)
XLA Ops:
  15.7 5.5 convolution_convert_fusion
  21.2 6.6 copy.76
  27.9 5.7 copy.113
  52.0 14.6 collective-permute-done.2
  66.6 25.4 %collective-permute-done.1 = bf16[8,128,3,192]{1,3,2,0:T(8,128)(2,1)} collective-permute-done((bf16[8,128,3,192]{1,3,2,0:T(8,128)(2,1)}, bf16[8,128,3,192]{1,3,2,0:T(8,128)(2,1)}, u32[]{:S(2)}, u32[]{:S(2)}) %collective-permute-start.1) | collective-permute-done | bytes 1179680 | tf_op jit(solution)/shard_map/ppermute | solution.py:28
  96.0 5.6 gather_fusion
  107.0 10.6 select_reduce_fusion
  117.6 11.4 fusion
  129.0 12.6 fusion.62
  158.7 5.5 gather_fusion.6
  168.7 5.5 gather_fusion.5
  193.2 5.5 gather_fusion.4
  198.8 5.5 gather_fusion.2
  204.3 23.4 %multiply_convert_fusion.1 = (bf16[640,3072]{1,0:T(8,128)(2,1)}, f32[640,3072]{1,0:T(8,128)}, f32[640,3072]{1,0:T(8,128)}) fusion(bf16[640,768]{1,0:T(8,128)(2,1)} %gather_fusion.4, bf16[2,768,3072]{2,1,0:T(8,128)(2,1)} %param.21), kind=kOutput, calls=%fused_computation.32 | convolution fusion | flops 3147694080 | bytes 25362432 | tf_op jit(solution)/shard_map/dot_general | solution.py:123
  227.7 22.7 %multiply_convert_fusion.2 = (bf16[640,3072]{1,0:T(8,128)(2,1)}, f32[640,3072]{1,0:T(8,128)}, f32[640,3072]{1,0:T(8,128)}) fusion(bf16[640,768]{1,0:T(8,128)(2,1)S(1)} %copy-done.23, bf16[2,768,3072]{2,1,0:T(8,128)(2,1)} %param.21), kind=kOutput, calls=%fused_computation.45 | convolution fusion | flops 3147694080 | bytes 25362432 | tf_op jit(solution)/shard_map/dot_general | solution.py:123
  250.4 10.0 add_convert_fusion
  265.1 9.9 add_convert_fusion.1
  281.4 9.8 scatter_custom_fusion.2
  291.2 11.7 scatter_fusion
  328.7 13.5 all-to-all-done.1
  350.2 20.0 %multiply_reduce_fusion = (f32[8,3,512]{2,1,0:T(4,128)S(1)}, f32[8,3,512,512]{2,3,1,0:T(8,128)}) fusion(f32[8,3,512,512]{2,3,1,0:T(8,128)} %get-tuple-element.60, f32[8,3,512]{2,1,0:T(4,128)} %log_add_fusion, pred[8,512,512]{1,2,0:T(8,128)(4,1)} %broadcast_compare_fusion, bf16[8,512,3,64]{1,3,2,0:T(8,128)(2,1)} %reshape.238, ...), kind=kOutput, calls=%fused_computation.12 | convolution fusion | flops 830459904 | bytes 55672832 | tf_op jit(solution)/shard_map/rqhc,rkhc->rhqk/dot_general | solution.py:172
  370.2 17.6 %multiply_convert_fusion = bf16[8,3,512,512]{2,3,1,0:T(8,128)(2,1)S(1)} fusion(f32[8,3,512,512]{2,3,1,0:T(8,128)} %get-tuple-element.66, f32[8,3,512,512]{2,3,1,0:T(8,128)} %get-tuple-element.60, f32[8,3,512]{2,1,0:T(4,128)S(1)} %get-tuple-element.65, f32[8,3,512]{2,1,0:T(4,128)S(1)} %copy-done.31, pred[8,512,512]{1,2,0:T(8,128)(4,1)S(1)} %copy-done.7), kind=kLoop, calls=%fused_computation.11 | loop fusion | flops 31457280 | bytes 65110016 | tf_op jit(solution)/shard_map/convert_element_type | solution.py:175
  395.7 9.8 convolution_convert_fusion.1
  405.6 13.1 fusion.63
  431.9 6.7 pad_maximum_fusion.2
  438.7 5.2 all-to-all-start.2
  447.6 67.0 %all-to-all-done.2 = bf16[8,512,3,192]{3,0,2,1:T(8,128)(2,1)} async-done(((bf16[8,512,3,192]{3,0,2,1:T(8,128)(2,1)}), bf16[8,512,3,192]{3,0,2,1:T(8,128)(2,1)}, u32[]{:S(2)}, u32[]{:S(2)}) %all-to-all-start.2) | async-done | bytes 4718624 | tf_op jit(solution)/shard_map/all_to_all | solution.py:191
  514.6 8.6 copy.103
  523.2 5.5 copy.96
  530.8 5.9 fusion.20
  537.0 6.4 convolution_bitcast_fusion.2
  547.4 6.9 pad_maximum_fusion
  555.0 6.5 convolution_bitcast_fusion
  565.6 6.9 pad_maximum_fusion.1
  582.3 11.0 select_reduce_fusion.8
  601.3 8.2 fusion.34
  611.1 55.8 %reduce-scatter.17.cloned.1.call-done = f32[96,2304]{1,0:T(8,128)} async-done(((f32[768,2304]{1,0:T(8,128)}), f32[96,2304]{1,0:T(8,128)}) %reduce-scatter.17.cloned.1.call-update) | async-done | bytes 884752 | tf_op jit(solution)/shard_map/reduce_scatter | solution.py:203
  668.8 310.7 %reduce-scatter.21.cloned.1.call-done = f32[2,96,3072]{2,1,0:T(8,128)} async-done(((f32[2,768,3072]{2,1,0:T(8,128)}), f32[2,96,3072]{2,1,0:T(8,128)}) %reduce-scatter.21.cloned.1.call-update) | async-done | bytes 2359312 | tf_op jit(solution)/shard_map/reduce_scatter | solution.py:207
  982.4 309.7 %reduce-scatter.23.cloned.1.call-done = f32[2,384,768]{2,1,0:T(8,128)} async-done(((f32[2,3072,768]{2,1,0:T(8,128)}), f32[2,384,768]{2,1,0:T(8,128)}) %reduce-scatter.23.cloned.1.call-update) | async-done | bytes 2359312 | tf_op jit(solution)/shard_map/reduce_scatter | solution.py:208
  1294.9 8.0 fusion.26
  1302.9 12.2 scatter_custom_fusion
  1315.2 12.1 scatter_custom_fusion.1
  1327.2 29.3 %reduce-scatter.31.cloned.1.call-done = f32[96,2]{1,0:T(8,128)} async-done(((f32[768,2]{1,0:T(8,128)}), f32[96,2]{1,0:T(8,128)}) %reduce-scatter.31.cloned.1.call-update) | async-done | bytes 784
  1357.9 63.0 %reduce-scatter.29.cloned.1.call-done = f32[96,2]{1,0:T(8,128)} async-done(((f32[768,2]{1,0:T(8,128)}), f32[96,2]{1,0:T(8,128)}) %reduce-scatter.29.cloned.1.call-update) | async-done | bytes 784
  1428.9 56.4 %reduce-scatter.27.cloned.1.call-done = f32[96,2]{1,0:T(8,128)} async-done(((f32[768,2]{1,0:T(8,128)}), f32[96,2]{1,0:T(8,128)}) %reduce-scatter.27.cloned.1.call-update) | async-done | bytes 784
  1486.2 63.7 %reduce-scatter.25.cloned.1.call-done = f32[96,2]{1,0:T(8,128)} async-done(((f32[768,2]{1,0:T(8,128)}), f32[96,2]{1,0:T(8,128)}) %reduce-scatter.25.cloned.1.call-update) | async-done | bytes 784
  1550.8 6.2 all-reduce
  1561.9 55.6 %all-reduce.4.cloned.1.call-done = (bf16[96,2304]{1,0:T(8,128)(2,1)}, bf16[96,768]{1,0:T(8,128)(2,1)}, bf16[2,96,3072]{2,1,0:T(8,128)(2,1)}, bf16[2,384,768]{2,1,0:T(8,128)(2,1)}) async-done(((bf16[96,2304]{1,0:T(8,128)(2,1)}, bf16[96,768]{1,0:T(8,128)(2,1)}, bf16[2,96,3072]{2,1,0:T(8,128)(2,1)}, bf16[2,384,768]{2,1,0:T(8,128)(2,1)}), (bf16[96,2304]{1,0:T(8,128)(2,1)}, bf16[96,768]{1,0:T(8,128)(2,1)}, ...) | async-done | bytes 2949136 | tf_op jit(solution)/shard_map/psum | solution.py:213
  (273 shorter events, 207.5 us)
Async XLA Ops:
  7.2 8.5 copy-start
  37.5 29.1 %collective-permute-start.2 = (bf16[8,128,3,192]{1,3,2,0:T(8,128)(2,1)}, bf16[8,128,3,192]{1,3,2,0:T(8,128)(2,1)}, u32[]{:S(2)}, u32[]{:S(2)}) collective-permute-start(bf16[8,128,3,192]{1,3,2,0:T(8,128)(2,1)} %bitcast.181), channel_id=1, source_target_pairs={{0,3},{1,2},{2,1},{3,0},{4,7},{5,6},{6,5},{7,4},{8,11},{9,10},{10,... | collective-permute-start | bytes 3538952 | tf_op jit(solution)/shard_map/ppermute | solution.py:28
  41.2 25.4 %collective-permute-start = (bf16[8,128,3,192]{1,3,2,0:T(8,128)(2,1)}, bf16[8,128,3,192]{1,3,2,0:T(8,128)(2,1)}, u32[]{:S(2)}, u32[]{:S(2)}) collective-permute-start(bf16[8,128,3,192]{1,3,2,0:T(8,128)(2,1)} %bitcast.183), channel_id=1, source_target_pairs={{0,1},{1,0},{2,3},{3,2},{4,5},{5,4},{6,7},{7,6},{8,9},{9,8},{10,11... | collective-permute-start | bytes 3538952 | tf_op jit(solution)/shard_map/ppermute | solution.py:28
  43.1 48.9 %collective-permute-start.1 = (bf16[8,128,3,192]{1,3,2,0:T(8,128)(2,1)}, bf16[8,128,3,192]{1,3,2,0:T(8,128)(2,1)}, u32[]{:S(2)}, u32[]{:S(2)}) collective-permute-start(bf16[8,128,3,192]{1,3,2,0:T(8,128)(2,1)} %bitcast.182), channel_id=1, source_target_pairs={{0,2},{1,3},{2,0},{3,1},{4,6},{5,7},{6,4},{7,5},{8,10},{9,11},{10,... | collective-permute-start | bytes 3538952 | tf_op jit(solution)/shard_map/ppermute | solution.py:28
  105.0 12.6 copy-start.10
  105.0 12.6 copy-start.12
  105.0 24.0 %copy-start.17 = (bf16[8,512,1,192]{1,3,2,0:T(8,128)(2,1)}, bf16[8,512,1,192]{1,3,2,0:T(8,128)(2,1)S(1)}, u32[]{:S(2)}) copy-start(bf16[8,512,1,192]{1,3,2,0:T(8,128)(2,1)S(1)} %get-tuple-element.48) | copy-start | bytes 4718596
  117.6 11.4 copy-start.30
  129.0 12.6 copy-start.33
  145.9 32.2 %all-to-all-start = ((bf16[8,512,192]{2,0,1:T(8,128)(2,1)}), bf16[8,512,192]{2,0,1:T(8,128)(2,1)}, u32[]{:S(2)}, u32[]{:S(2)}) async-start(bf16[8,512,192]{2,0,1:T(8,128)(2,1)} %copy.83), calls=%async_computation | async-start | bytes 4194304 | tf_op jit(solution)/shard_map/all_to_all | solution.py:107
  150.5 13.8 copy-start.51
  175.6 14.6 copy-start.39
  175.6 14.6 copy-start.41
  184.3 6.6 copy-start.59
  184.3 6.6 copy-start.62
  184.3 6.6 copy-start.63
  204.3 23.4 %copy-start.23 = (bf16[640,768]{1,0:T(8,128)(2,1)S(1)}, bf16[640,768]{1,0:T(8,128)(2,1)}, u32[]{:S(2)}) copy-start(bf16[640,768]{1,0:T(8,128)(2,1)} %gather_fusion.2) | copy-start | bytes 2949124
  204.3 56.2 %slice-start = ((s8[9437184]{0:T(1024)(128)(4,1)}), s8[4194304]{0:T(1024)(128)(4,1)S(1)}, s32[]{:S(2)}) async-start(s8[9437184]{0:T(1024)(128)(4,1)} %bitcast.219), calls=%async_computation.20 | async-start | bytes 8388608
  204.3 56.2 %slice-start.1 = ((s8[9437184]{0:T(1024)(128)(4,1)}), s8[4194304]{0:T(1024)(128)(4,1)S(1)}, s32[]{:S(2)}) async-start(s8[9437184]{0:T(1024)(128)(4,1)} %bitcast.219), calls=%async_computation.21 | async-start | bytes 8388608
  227.7 22.7 %copy-start.27 = (bf16[640,768]{1,0:T(8,128)(2,1)S(1)}, bf16[640,768]{1,0:T(8,128)(2,1)}, u32[]{:S(2)}) copy-start(bf16[640,768]{1,0:T(8,128)(2,1)} %gather_fusion.6) | copy-start | bytes 2949124
  227.7 22.7 %copy-start.65 = (pred[640]{0:T(1024)(128)(4,1)S(1)}, pred[640]{0:T(1024)(128)(4,1)}, u32[]{:S(2)}) copy-start(pred[640]{0:T(1024)(128)(4,1)} %broadcast_compare_fusion.3) | copy-start | bytes 1924
  227.7 32.8 %slice-start.2 = ((s8[9437184]{0:T(1024)(128)(4,1)}), s8[1048576]{0:T(1024)(128)(4,1)S(1)}, s32[]{:S(2)}) async-start(s8[9437184]{0:T(1024)(128)(4,1)} %bitcast.219), calls=%async_computation.22 | async-start | bytes 2097152
  291.2 11.7 copy-start.36
  291.2 11.7 copy-start.40
  291.2 11.7 copy-start.42
  291.2 11.7 copy-start.44
  317.6 24.7 %all-to-all-start.1 = ((bf16[8,128,768]{1,0,2:T(8,128)(2,1)}), bf16[8,128,768]{1,0,2:T(8,128)(2,1)}, u32[]{:S(2)}, u32[]{:S(2)}) async-start(bf16[8,128,768]{1,0,2:T(8,128)(2,1)} %copy.86), calls=%async_computation.1 | async-start | bytes 3145728 | tf_op jit(solution)/shard_map/all_to_all | solution.py:169
  322.0 287.5 %reduce-scatter.19.cloned.1.call-start = ((), (), s32[]{:S(2)}) async-start(), calls=%async_computation.12 | async-start | bytes 2654208 | tf_op jit(solution)/shard_map/reduce_scatter | solution.py:204
  350.2 20.0 %copy-start.7 = (pred[8,512,512]{1,2,0:T(8,128)(4,1)S(1)}, pred[8,512,512]{1,2,0:T(8,128)(4,1)}, u32[]{:S(2)}) copy-start(pred[8,512,512]{1,2,0:T(8,128)(4,1)} %broadcast_compare_fusion) | copy-start | bytes 6291460
  350.2 20.0 %copy-start.31 = (f32[8,3,512]{2,1,0:T(4,128)S(1)}, f32[8,3,512]{2,1,0:T(4,128)}, u32[]{:S(2)}) copy-start(f32[8,3,512]{2,1,0:T(4,128)} %log_add_fusion) | copy-start | bytes 147460
  370.2 22.2 %copy-start.13 = (bf16[8,512,1,192]{1,3,2,0:T(8,128)(2,1)S(1)}, bf16[8,512,1,192]{1,3,2,0:T(8,128)(2,1)}, u32[]{:S(2)}) copy-start(bf16[8,512,1,192]{1,3,2,0:T(8,128)(2,1)} %copy-done.12) | copy-start | bytes 4718596
  395.7 9.8 copy-start.18
  438.7 75.9 %all-to-all-start.2 = ((bf16[8,512,3,192]{3,0,2,1:T(8,128)(2,1)}), bf16[8,512,3,192]{3,0,2,1:T(8,128)(2,1)}, u32[]{:S(2)}, u32[]{:S(2)}) async-start(bf16[8,512,3,192]{3,0,2,1:T(8,128)(2,1)} %pad_maximum_fusion.2), calls=%async_computation.2 | async-start | bytes 12582912 | tf_op jit(solution)/shard_map/all_to_all | solution.py:191
  443.9 222.9 %reduce-scatter.17.cloned.1.call-start = ((), (), s32[]{:S(2)}) async-start(), calls=%async_computation.11 | async-start | bytes 7962624 | tf_op jit(solution)/shard_map/reduce_scatter | solution.py:203
  523.2 7.7 copy-start.26
  536.8 442.8 %reduce-scatter.21.cloned.1.call-start = ((), (), s32[]{:S(2)}) async-start(), calls=%async_computation.13 | async-start | bytes 21233664 | tf_op jit(solution)/shard_map/reduce_scatter | solution.py:207
  554.4 737.7 %reduce-scatter.23.cloned.1.call-start = ((), (), s32[]{:S(2)}) async-start(), calls=%async_computation.14 | async-start | bytes 21233664 | tf_op jit(solution)/shard_map/reduce_scatter | solution.py:208
  555.0 6.5 copy-start.68
  555.0 6.5 copy-start.72
  572.5 9.7 copy-start.53
  572.6 783.9 %reduce-scatter.31.cloned.1.call-start = ((), (), s32[]{:S(2)}) async-start(), calls=%async_computation.18 | async-start | bytes 442368
  578.7 842.1 %reduce-scatter.29.cloned.1.call-start = ((), (), s32[]{:S(2)}) async-start(), calls=%async_computation.17 | async-start | bytes 442368
  581.7 903.6 %reduce-scatter.27.cloned.1.call-start = ((), (), s32[]{:S(2)}) async-start(), calls=%async_computation.16 | async-start | bytes 442368
  598.1 951.9 %reduce-scatter.25.cloned.1.call-start = ((), (), s32[]{:S(2)}) async-start(), calls=%async_computation.15 | async-start | bytes 442368
  601.1 1016.4 %all-reduce.4.cloned.1.call-start = ((), (), s32[]{:S(2)}) async-start(), calls=%async_computation.19 | async-start | bytes 5898240 | tf_op jit(solution)/shard_map/psum | solution.py:213
  1426.8 124.0 %copy-start.69 = (bf16[2,96]{1,0:T(2,128)(2,1)S(1)}, bf16[2,96]{1,0:T(2,128)(2,1)}, u32[]{:S(2)}) copy-start(bf16[2,96]{1,0:T(2,128)(2,1)} %copy.111) | copy-start | bytes 1156
  1426.9 124.0 %copy-start.70 = (bf16[2,96]{1,0:T(2,128)(2,1)S(1)}, bf16[2,96]{1,0:T(2,128)(2,1)}, u32[]{:S(2)}) copy-start(bf16[2,96]{1,0:T(2,128)(2,1)} %copy.109) | copy-start | bytes 1156
  1617.5 6.8 copy-start.34
  (43 other events, 144.9 us)
Sparse Core Ops, SparseCore 0:
  328.9 72.0 reduce-scatter.18
  536.9 129.9 reduce-scatter.16
  670.7 308.7 reduce-scatter.20
  983.3 308.7 reduce-scatter.22
  1295.2 61.2 reduce-scatter.30
  1359.6 61.1 reduce-scatter.28
  1424.1 61.1 reduce-scatter.26
  1488.6 61.2 reduce-scatter.24
  1553.1 64.3 all-reduce.3
